TPU v7x, 256 devices: a whole 4x4x8 slice. The times are simulated.
256 devices in a mesh: dp: 32 (over z_hi, x, core), seq: 8 (over y, z_lo).
Axes of the slice: x: 4, y: 4, z: 8 (z_hi: 4, z_lo: 2; z = z_hi * 2 + z_lo), core: 2. Of those that a mesh axis runs over, the one named last changes fastest.
Arguments:
- q_proj: bfloat16 [32, 1024, 4096], P('dp', 'seq'), may hold values from -200 to 200
- k_proj: bfloat16 [32, 1024, 512], P('dp', 'seq'), may hold values from -6 to 6
- v_proj: bfloat16 [32, 1024, 512], P('dp', 'seq'), may hold values from -6 to 6
- cache_k: bfloat16 [32, 1024, 512], P('dp', 'seq'), may hold values from -6 to 6
- cache_v: bfloat16 [32, 1024, 512], P('dp', 'seq'), may hold values from -6 to 6
- bias_q: bfloat16 [4096], replicated, may hold values from -3 to 3
- bias_k: bfloat16 [512], replicated, may hold values from -3 to 3
- bias_v: bfloat16 [512], replicated, may hold values from -3 to 3
- start: int32 [32], P('dp'), may hold values from 256 to 1024, as said below
- dout: bfloat16 [32, 1024, 4096], P('dp', 'seq'), may hold values from -6 to 6
Outputs:
- attn_out: bfloat16 [32, 1024, 4096], P('dp', 'seq')
- grad_q: bfloat16 [32, 1024, 4096], P('dp', 'seq')
- grad_k: bfloat16 [32, 1024, 512], P('dp', 'seq')
- grad_v: bfloat16 [32, 1024, 512], P('dp', 'seq')
- grad_bias_q: float32 [4096], replicated
- grad_bias_k: float32 [512], replicated
- grad_bias_v: float32 [512], replicated
Inputs may be any that keep to these rules, and one draw needn't show every extreme that they name: Cache slots at and beyond start hold no prefix; some sequence has a full prefix of 1024 slots.
All inputs are finite; a program needn't handle non-finite values.
Results may differ from a plain program's by a relative error of at most 0.04.
The roundings to bfloat16 on the way count: a program that leaves them out, or rounds other values in their place, can miss the bound.
Values may be sent and summed in bfloat16 or wider, within the bound.
A program may use at most 128 MiB of HBM per device.

v0:
```python
import jax
import jax.numpy as jnp
from jax import lax
from jax.sharding import PartitionSpec as P

HQ = 32
KV = 4
HD = 128
GROUP = 8


def rotary_tables(positions, width):
    half = width // 2
    freqs = jnp.exp(
        -(2.0 * jnp.arange(half, dtype=jnp.float32) / width) * jnp.log(jnp.float32(1000000.0))
    )
    angles = positions.astype(jnp.float32)[:, None] * freqs[None, :]
    cosine = jnp.concatenate([jnp.cos(angles), jnp.cos(angles)], axis=1)
    sine = jnp.concatenate([jnp.sin(angles), jnp.sin(angles)], axis=1)
    return (cosine[:, None, :], sine[:, None, :])


def rotary(values, positions):
    cosine, sine = rotary_tables(positions, values.shape[2])
    half = values.shape[2] // 2
    turned = jnp.concatenate([-values[:, :, half:], values[:, :, :half]], axis=2)
    return values * cosine + turned * sine


def rotary_back(grads, positions):
    cosine, sine = rotary_tables(positions, grads.shape[2])
    half = grads.shape[2] // 2
    scaled = grads * sine
    turned = jnp.concatenate([scaled[:, :, half:], -scaled[:, :, :half]], axis=2)
    return grads * cosine + turned


def attend(queries, cotangent, keys, values, first, row_zero, prefix):
    rows, heads, width = queries.shape
    key_count = keys.shape[0]
    slab = key_count - prefix
    head_block = max(1, min(512 // rows, GROUP, heads))
    row_block = min(rows, 512)
    scale = width ** (-0.5)
    key_index = jnp.arange(key_count, dtype=jnp.int32)

    def head_step(carry, head_slot):
        key_acc, value_acc = carry
        head_zero = head_slot * head_block
        owner = head_zero // GROUP
        key_one = lax.dynamic_index_in_dim(keys, owner, 1, keepdims=False)
        value_one = lax.dynamic_index_in_dim(values, owner, 1, keepdims=False)
        query_part = lax.dynamic_slice_in_dim(queries, head_zero, head_block, 1)
        cot_part = lax.dynamic_slice_in_dim(cotangent, head_zero, head_block, 1)

        def row_step(inner, row_slot):
            grad_key, grad_value = inner
            offset = row_slot * row_block
            query_rows = lax.dynamic_slice_in_dim(query_part, offset, row_block, 0)
            cot_rows = lax.dynamic_slice_in_dim(cot_part, offset, row_block, 0)
            query_index = row_zero + offset + jnp.arange(row_block, dtype=jnp.int32)
            allowed = jnp.where(
                key_index[None, :] < prefix,
                key_index[None, :] < first,
                key_index[None, :] - prefix <= query_index[:, None],
            )
            scores = (
                jnp.einsum("rhd,kd->hrk", query_rows, key_one, preferred_element_type=jnp.float32)
                * scale
            )
            scores = jnp.where(allowed[None], scores, -1e30)
            highest = jnp.max(scores, axis=-1, keepdims=True)
            expo = jnp.exp(scores - highest)
            probs = expo / jnp.sum(expo, axis=-1, keepdims=True)
            probs_b = probs.astype(jnp.bfloat16)
            output = jnp.einsum(
                "hrk,kd->rhd", probs_b, value_one, preferred_element_type=jnp.float32
            ).astype(jnp.bfloat16)
            delta = jnp.sum(cot_rows.astype(jnp.float32) * output.astype(jnp.float32), axis=-1).T
            dprobs = jnp.einsum(
                "rhd,kd->hrk", cot_rows, value_one, preferred_element_type=jnp.float32
            )
            dscore = (probs * (dprobs - delta[:, :, None])).astype(jnp.bfloat16)
            grad_query = (
                jnp.einsum("hrk,kd->rhd", dscore, key_one, preferred_element_type=jnp.float32)
                * scale
            ).astype(jnp.bfloat16)
            grad_key = (
                grad_key
                + jnp.einsum(
                    "hrk,rhd->kd",
                    dscore[:, :, prefix:],
                    query_rows,
                    preferred_element_type=jnp.float32,
                )
                * scale
            )
            grad_value = grad_value + jnp.einsum(
                "hrk,rhd->kd", probs_b[:, :, prefix:], cot_rows, preferred_element_type=jnp.float32
            )
            return ((grad_key, grad_value), (output, grad_query))

        empty = jnp.zeros((slab, width), jnp.float32)
        (grad_key, grad_value), (outputs, grads) = lax.scan(
            row_step, (empty, empty), jnp.arange(rows // row_block, dtype=jnp.int32)
        )
        outputs = outputs.reshape(rows, head_block, width)
        grads = grads.reshape(rows, head_block, width)
        old_key = lax.dynamic_index_in_dim(key_acc, owner, 1, keepdims=False)
        old_value = lax.dynamic_index_in_dim(value_acc, owner, 1, keepdims=False)
        key_acc = lax.dynamic_update_index_in_dim(key_acc, old_key + grad_key, owner, 1)
        value_acc = lax.dynamic_update_index_in_dim(value_acc, old_value + grad_value, owner, 1)
        return ((key_acc, value_acc), (outputs, grads))

    zeros_kv = jnp.zeros((slab, keys.shape[1], width), jnp.float32)
    (key_acc, value_acc), (outputs, grads) = lax.scan(
        head_step, (zeros_kv, zeros_kv), jnp.arange(heads // head_block, dtype=jnp.int32)
    )
    outputs = jnp.transpose(outputs, (1, 0, 2, 3)).reshape(rows, heads, width)
    grads = jnp.transpose(grads, (1, 0, 2, 3)).reshape(rows, heads, width)
    return (outputs, grads, key_acc, value_acc)


def body(q_proj, k_proj, v_proj, cache_k, cache_v, bias_q, bias_k, bias_v, start, dout):
    devices = lax.axis_size("seq")
    rank = lax.axis_index("seq")
    tokens = q_proj.shape[1]
    first = start[0]
    positions = first + rank * tokens + jnp.arange(tokens, dtype=jnp.int32)
    queries = rotary(
        (q_proj[0].astype(jnp.float32) + bias_q.astype(jnp.float32)).reshape(tokens, HQ, HD),
        positions,
    ).astype(jnp.bfloat16)
    keys = rotary(
        (k_proj[0].astype(jnp.float32) + bias_k.astype(jnp.float32)).reshape(tokens, KV, HD),
        positions,
    ).astype(jnp.bfloat16)
    values = (
        (v_proj[0].astype(jnp.float32) + bias_v.astype(jnp.float32))
        .astype(jnp.bfloat16)
        .reshape(tokens, KV, HD)
    )
    cotangent = dout[0].reshape(tokens, HQ, HD)
    cached_keys = cache_k[0].reshape(cache_k.shape[1], KV, HD)
    cached_values = cache_v[0].reshape(cache_v.shape[1], KV, HD)
    copies = max(devices // KV, 1)
    keys_wide = jnp.repeat(keys, copies, axis=1)
    values_wide = jnp.repeat(values, copies, axis=1)
    cache_keys_wide = jnp.repeat(cached_keys, copies, axis=1)
    cache_values_wide = jnp.repeat(cached_values, copies, axis=1)
    head_queries, head_keys, head_values, head_cot = (
        lax.all_to_all(queries, "seq", split_axis=1, concat_axis=0, tiled=True),
        lax.all_to_all(keys_wide, "seq", split_axis=1, concat_axis=0, tiled=True),
        lax.all_to_all(values_wide, "seq", split_axis=1, concat_axis=0, tiled=True),
        lax.all_to_all(cotangent, "seq", split_axis=1, concat_axis=0, tiled=True),
    )
    head_cache_keys, head_cache_values = (
        lax.all_to_all(cache_keys_wide, "seq", split_axis=1, concat_axis=0, tiled=True),
        lax.all_to_all(cache_values_wide, "seq", split_axis=1, concat_axis=0, tiled=True),
    )
    prefix = head_cache_keys.shape[0]
    all_keys = jnp.concatenate([head_cache_keys, head_keys], axis=0)
    all_values = jnp.concatenate([head_cache_values, head_values], axis=0)
    outputs, dq_rot, dk_rot, dv_all = attend(
        head_queries, head_cot, all_keys, all_values, first, 0, prefix
    )
    out_tokens, dq_tokens = (
        lax.all_to_all(outputs, "seq", split_axis=0, concat_axis=1, tiled=True),
        lax.all_to_all(dq_rot, "seq", split_axis=0, concat_axis=1, tiled=True),
    )
    dk_copies, dv_copies = (
        lax.all_to_all(
            dk_rot.astype(jnp.bfloat16), "seq", split_axis=0, concat_axis=1, tiled=True
        ).astype(dk_rot.dtype),
        lax.all_to_all(
            dv_all.astype(jnp.bfloat16), "seq", split_axis=0, concat_axis=1, tiled=True
        ).astype(dv_all.dtype),
    )
    dk_tokens = jnp.sum(dk_copies.reshape(tokens, KV, copies, HD), axis=2)
    dv_tokens = jnp.sum(dv_copies.reshape(tokens, KV, copies, HD), axis=2)
    grad_query = rotary_back(dq_tokens.astype(jnp.float32), positions)
    grad_key = rotary_back(dk_tokens, positions)
    sums_query, sums_key, sums_value = lax.psum(
        (
            jnp.sum(grad_query, axis=0).reshape(HQ * HD),
            jnp.sum(grad_key, axis=0).reshape(KV * HD),
            jnp.sum(dv_tokens, axis=0).reshape(KV * HD),
        ),
        ("dp", "seq"),
    )
    return (
        out_tokens.reshape(1, tokens, HQ * HD),
        grad_query.astype(jnp.bfloat16).reshape(1, tokens, HQ * HD),
        grad_key.astype(jnp.bfloat16).reshape(1, tokens, KV * HD),
        dv_tokens.astype(jnp.bfloat16).reshape(1, tokens, KV * HD),
        sums_query,
        sums_key,
        sums_value,
    )


def solution(mesh):
    placed = (
        P("dp", "seq", None),
        P("dp", "seq", None),
        P("dp", "seq", None),
        P("dp", "seq", None),
        P("dp", "seq", None),
        P(),
        P(),
        P(),
        P("dp"),
        P("dp", "seq", None),
    )
    return jax.shard_map(
        body,
        mesh=mesh,
        in_specs=placed,
        out_specs=(
            P("dp", "seq", None),
            P("dp", "seq", None),
            P("dp", "seq", None),
            P("dp", "seq", None),
            P(),
            P(),
            P(),
        ),
        check_vma=False,
    )
```

profile of v0, /device:TPU:1, one launch (start us, length us, event | category | flops | bytes accessed | tf_op | source)
XLA Modules:
  0.0 376.5 jit_solution(17324488417311112449)
XLA Ops:
  2.4 6.5 %all-to-all-start.2 = ((bf16[128,8,128]{2,0,1:T(8,128)(2,1)}), bf16[128,8,128]{2,0,1:T(8,128)(2,1)S(1)}, u32[]{:S(2)}, u32[]{:S(2)}) async-start(bf16[128,8,128]{2,0,1:T(8,128)(2,1)} %bitcast.11), calls=%async_computation.2 | async-start | bytes 524288 | tf_op jit(solution)/shard_map/all_to_all | solution.py:158
  15.8 3.4 all-to-all-start.4
  19.3 6.0 %all-to-all-done.4 = bf16[128,8,128]{2,0,1:T(8,128)(2,1)S(1)} async-done(((bf16[128,8,128]{2,0,1:T(8,128)(2,1)}), bf16[128,8,128]{2,0,1:T(8,128)(2,1)S(1)}, u32[]{:S(2)}, u32[]{:S(2)}) %all-to-all-start.4) | async-done | bytes 262176 | tf_op jit(solution)/shard_map/all_to_all | solution.py:159
  26.1 3.4 all-to-all-start.5
  29.8 5.8 %all-to-all-done.5 = bf16[128,8,128]{2,0,1:T(8,128)(2,1)S(1)} async-done(((bf16[128,8,128]{2,0,1:T(8,128)(2,1)}), bf16[128,8,128]{2,0,1:T(8,128)(2,1)S(1)}, u32[]{:S(2)}, u32[]{:S(2)}) %all-to-all-start.5) | async-done | bytes 262176 | tf_op jit(solution)/shard_map/all_to_all | solution.py:154
  36.4 3.4 all-to-all-start.3
  41.2 4.7 %all-to-all-done.3 = bf16[128,8,128]{2,0,1:T(8,128)(2,1)S(1)} async-done(((bf16[128,8,128]{2,0,1:T(8,128)(2,1)}), bf16[128,8,128]{2,0,1:T(8,128)(2,1)S(1)}, u32[]{:S(2)}, u32[]{:S(2)}) %all-to-all-start.3) | async-done | bytes 262176 | tf_op jit(solution)/shard_map/all_to_all | solution.py:153
  45.9 3.7 all-to-all-start.1
  53.5 6.5 %all-to-all-done.1 = bf16[128,32,128]{0,2,1:T(8,128)(2,1)S(1)} async-done(((bf16[128,32,128]{0,2,1:T(8,128)(2,1)}), bf16[128,32,128]{0,2,1:T(8,128)(2,1)S(1)}, u32[]{:S(2)}, u32[]{:S(2)}) %all-to-all-start.1) | async-done | bytes 1048608 | tf_op jit(solution)/shard_map/all_to_all | solution.py:155
  60.0 3.6 all-to-all-start
  66.7 7.2 %all-to-all-done = bf16[128,32,128]{2,0,1:T(8,128)(2,1)S(1)} async-done(((bf16[128,32,128]{2,0,1:T(8,128)(2,1)}), bf16[128,32,128]{2,0,1:T(8,128)(2,1)S(1)}, u32[]{:S(2)}, u32[]{:S(2)}) %all-to-all-start) | async-done | bytes 1048608 | tf_op jit(solution)/shard_map/all_to_all | solution.py:152
  75.0 139.6 %while.59 = (s32[]{:T(128)}, f32[1024,1,128]{2,0,1:T(8,128)S(1)}, f32[1024,1,128]{2,0,1:T(8,128)S(1)}, bf16[4,1024,1,128]{3,1,2,0:T(8,128)(2,1)}, bf16[4,1024,1,...) while((s32[]{:T(128)}, f32[1024,1,128]{2,0,1:T(8,128)S(1)}, ...), condition=%wide.region_6.7_spmd.clone.clone, body=%wide.region_0.6_spmd.clone.clone.sunk | while | flops 1359287296 | bytes 49224388 | solution.py:116
  79.6 28.5 %while.60 = (s32[]{:T(128)}, f32[1024,128]{1,0:T(8,128)S(1)}, f32[1024,128]{1,0:T(8,128)S(1)}, bf16[2,512,1,128]{3,1,0,2:T(8,128)(2,1)}, bf16[2,512,1,128]{3,1,2...) while((s32[]{:T(128)}, f32[1024,128]{1,0:T(8,128)S(1)}, ...), condition=%wide.region_5.5_spmd.clone.clone, body=%wide.region_1.4_spmd.clone.clone.sunk | while | flops 1359025152 | bytes 41875732 | solution.py:104
  90.1 3.1 fusion.81
  104.4 3.1 fusion.81
  114.5 28.5 %while.60 = (s32[]{:T(128)}, f32[1024,128]{1,0:T(8,128)S(1)}, f32[1024,128]{1,0:T(8,128)S(1)}, bf16[2,512,1,128]{3,1,0,2:T(8,128)(2,1)}, bf16[2,512,1,128]{3,1,2...) while((s32[]{:T(128)}, f32[1024,128]{1,0:T(8,128)S(1)}, ...), condition=%wide.region_5.5_spmd.clone.clone, body=%wide.region_1.4_spmd.clone.clone.sunk | while | flops 1359025152 | bytes 41875732 | solution.py:104
  125.0 3.1 fusion.81
  139.3 3.1 fusion.81
  149.4 28.5 %while.60 = (s32[]{:T(128)}, f32[1024,128]{1,0:T(8,128)S(1)}, f32[1024,128]{1,0:T(8,128)S(1)}, bf16[2,512,1,128]{3,1,0,2:T(8,128)(2,1)}, bf16[2,512,1,128]{3,1,2...) while((s32[]{:T(128)}, f32[1024,128]{1,0:T(8,128)S(1)}, ...), condition=%wide.region_5.5_spmd.clone.clone, body=%wide.region_1.4_spmd.clone.clone.sunk | while | flops 1359025152 | bytes 41875732 | solution.py:104
  174.2 3.1 fusion.81
  184.3 28.5 %while.60 = (s32[]{:T(128)}, f32[1024,128]{1,0:T(8,128)S(1)}, f32[1024,128]{1,0:T(8,128)S(1)}, bf16[2,512,1,128]{3,1,0,2:T(8,128)(2,1)}, bf16[2,512,1,128]{3,1,2...) while((s32[]{:T(128)}, f32[1024,128]{1,0:T(8,128)S(1)}, ...), condition=%wide.region_5.5_spmd.clone.clone, body=%wide.region_1.4_spmd.clone.clone.sunk | while | flops 1359025152 | bytes 41875732 | solution.py:104
  209.1 3.1 fusion.81
  216.8 3.4 all-to-all-start.8
  221.8 4.5 %all-to-all-done.8 = bf16[8,2,8192]{2,1,0:T(2,128)(2,1)S(1)} async-done(((bf16[8,2,8192]{2,1,0:T(2,128)(2,1)}), bf16[8,2,8192]{2,1,0:T(2,128)(2,1)S(1)}, u32[]{:S(2)}, u32[]{:S(2)}) %all-to-all-start.8) | async-done | bytes 262176 | tf_op jit(solution)/shard_map/all_to_all | solution.py:172
  226.3 3.6 all-to-all-start.9
  229.9 3.1 copy.153
  233.0 3.2 all-to-all-done.9
  236.2 3.6 all-to-all-start.6
  241.6 9.9 %all-to-all-done.6 = bf16[1024,4,128]{2,1,0:T(4,128)(2,1)S(1)} async-done(((bf16[1024,4,128]{2,1,0:T(4,128)(2,1)}), bf16[1024,4,128]{2,1,0:T(4,128)(2,1)S(1)}, u32[]{:S(2)}, u32[]{:S(2)}) %all-to-all-start.6) | async-done | bytes 1048608 | tf_op jit(solution)/shard_map/all_to_all | solution.py:168
  251.5 3.6 all-to-all-start.7
  273.0 3.2 copy.163
  286.0 90.5 %all-reduce = (f32[4096]{0:T(1024)}, f32[512]{0:T(512)}, f32[512]{0:T(512)}) all-reduce(f32[4096]{0:T(1024)S(1)} %bitcast.274, f32[512]{0:T(512)S(1)} %bitcast.276, f32[512]{0:T(512)S(1)} %bitcast.277), channel_id=1, replica_groups=mesh['dp'=32,'seq'=8] {'dp','seq'}, use_global_device_ids=true, to_apply=%region_10.11 | all-reduce | flops 5120 | bytes 40960 | tf_op jit(solution)/shard_map/psum | solution.py:183
  (322 shorter events, 159.2 us)
Async XLA Ops:
  0.6 10.7 %copy-start.22 = (bf16[1,128,512]{2,1,0:T(8,128)(2,1)S(1)}, bf16[1,128,512]{2,1,0:T(8,128)(2,1)}, u32[]{:S(2)}) copy-start(bf16[1,128,512]{2,1,0:T(8,128)(2,1)} %param.15) | copy-start | bytes 393220
  0.6 10.9 %copy-start.23 = (bf16[1,128,512]{2,1,0:T(8,128)(2,1)S(1)}, bf16[1,128,512]{2,1,0:T(8,128)(2,1)}, u32[]{:S(2)}) copy-start(bf16[1,128,512]{2,1,0:T(8,128)(2,1)} %param.18) | copy-start | bytes 393220
  2.4 16.9 %copy-start.25 = (bf16[512]{0:T(512)(128)(2,1)S(1)}, bf16[512]{0:T(512)(128)(2,1)}, u32[]{:S(2)}) copy-start(bf16[512]{0:T(512)(128)(2,1)} %param.20) | copy-start | bytes 3076
  2.4 12.7 %all-to-all-start.2 = ((bf16[128,8,128]{2,0,1:T(8,128)(2,1)}), bf16[128,8,128]{2,0,1:T(8,128)(2,1)S(1)}, u32[]{:S(2)}, u32[]{:S(2)}) async-start(bf16[128,8,128]{2,0,1:T(8,128)(2,1)} %bitcast.11), calls=%async_computation.2 | async-start | bytes 524288 | tf_op jit(solution)/shard_map/all_to_all | solution.py:158
  12.1 37.5 %copy-start.8 = (f32[128,128]{1,0:T(8,128)}, f32[128,128]{1,0:T(8,128)S(1)}, u32[]{:S(2)}) copy-start(f32[128,128]{1,0:T(8,128)S(1)} %get-tuple-element.735) | copy-start | bytes 196612
  12.1 37.6 %copy-start.6 = (f32[128,128]{1,0:T(8,128)}, f32[128,128]{1,0:T(8,128)S(1)}, u32[]{:S(2)}) copy-start(f32[128,128]{1,0:T(8,128)S(1)} %get-tuple-element.734) | copy-start | bytes 196612
  15.8 9.5 %all-to-all-start.4 = ((bf16[128,8,128]{2,0,1:T(8,128)(2,1)}), bf16[128,8,128]{2,0,1:T(8,128)(2,1)S(1)}, u32[]{:S(2)}, u32[]{:S(2)}) async-start(bf16[128,8,128]{2,0,1:T(8,128)(2,1)} %bitcast.21), calls=%async_computation.4 | async-start | bytes 524288 | tf_op jit(solution)/shard_map/all_to_all | solution.py:159
  19.3 20.5 %copy-start.10 = (bf16[1,128,4096]{2,1,0:T(8,128)(2,1)S(1)}, bf16[1,128,4096]{2,1,0:T(8,128)(2,1)}, u32[]{:S(2)}) copy-start(bf16[1,128,4096]{2,1,0:T(8,128)(2,1)} %param.23) | copy-start | bytes 3145732
  25.3 15.8 %copy-start.13 = (bf16[128,8,128]{2,0,1:T(8,128)(2,1)}, bf16[128,8,128]{2,0,1:T(8,128)(2,1)S(1)}, u32[]{:S(2)}) copy-start(bf16[128,8,128]{2,0,1:T(8,128)(2,1)S(1)} %all-to-all-done.4) | copy-start | bytes 786436
  26.1 9.5 %all-to-all-start.5 = ((bf16[128,8,128]{2,0,1:T(8,128)(2,1)}), bf16[128,8,128]{2,0,1:T(8,128)(2,1)S(1)}, u32[]{:S(2)}, u32[]{:S(2)}) async-start(bf16[128,8,128]{2,0,1:T(8,128)(2,1)} %bitcast.26), calls=%async_computation.5 | async-start | bytes 524288 | tf_op jit(solution)/shard_map/all_to_all | solution.py:154
  36.4 9.5 %all-to-all-start.3 = ((bf16[128,8,128]{2,0,1:T(8,128)(2,1)}), bf16[128,8,128]{2,0,1:T(8,128)(2,1)S(1)}, u32[]{:S(2)}, u32[]{:S(2)}) async-start(bf16[128,8,128]{2,0,1:T(8,128)(2,1)} %bitcast.17), calls=%async_computation.3 | async-start | bytes 524288 | tf_op jit(solution)/shard_map/all_to_all | solution.py:153
  39.8 10.0 %copy-start.11 = (bf16[1,128,4096]{2,1,0:T(8,128)(2,1)S(1)}, bf16[1,128,4096]{2,1,0:T(8,128)(2,1)}, u32[]{:S(2)}) copy-start(bf16[1,128,4096]{2,1,0:T(8,128)(2,1)} %param.14) | copy-start | bytes 3145732
  45.9 3.8 %copy-start.17 = (bf16[128,8,128]{2,0,1:T(8,128)(2,1)}, bf16[128,8,128]{2,0,1:T(8,128)(2,1)S(1)}, u32[]{:S(2)}) copy-start(bf16[128,8,128]{2,0,1:T(8,128)(2,1)S(1)} %all-to-all-done.3) | copy-start | bytes 786436
  45.9 4.6 %copy-start.24 = (bf16[4096]{0:T(1024)(128)(2,1)S(1)}, bf16[4096]{0:T(1024)(128)(2,1)}, u32[]{:S(2)}) copy-start(bf16[4096]{0:T(1024)(128)(2,1)} %param.19) | copy-start | bytes 24580
  45.9 14.1 %all-to-all-start.1 = ((bf16[128,32,128]{0,2,1:T(8,128)(2,1)}), bf16[128,32,128]{0,2,1:T(8,128)(2,1)S(1)}, u32[]{:S(2)}, u32[]{:S(2)}) async-start(bf16[128,32,128]{0,2,1:T(8,128)(2,1)} %bitcast.6), calls=%async_computation.1 | async-start | bytes 2097152 | tf_op jit(solution)/shard_map/all_to_all | solution.py:155
  52.2 11.4 %copy-start.14 = (bf16[128,8,128]{2,0,1:T(8,128)(2,1)S(1)}, bf16[128,8,128]{2,0,1:T(8,128)(2,1)}, u32[]{:S(2)}) copy-start(bf16[128,8,128]{2,0,1:T(8,128)(2,1)} %copy-done.13) | copy-start | bytes 786436
  52.2 11.4 %copy-start.16 = (bf16[128,8,128]{2,0,1:T(8,128)(2,1)S(1)}, bf16[128,8,128]{2,0,1:T(8,128)(2,1)}, u32[]{:S(2)}) copy-start(bf16[128,8,128]{2,0,1:T(8,128)(2,1)} %copy-done.15) | copy-start | bytes 786436
  60.0 13.9 %all-to-all-start = ((bf16[128,32,128]{2,0,1:T(8,128)(2,1)}), bf16[128,32,128]{2,0,1:T(8,128)(2,1)S(1)}, u32[]{:S(2)}, u32[]{:S(2)}) async-start(bf16[128,32,128]{2,0,1:T(8,128)(2,1)} %copy.142), calls=%async_computation | async-start | bytes 2097152 | tf_op jit(solution)/shard_map/all_to_all | solution.py:152
  89.4 3.7 copy-start
  103.7 3.8 copy-start
  124.3 3.7 copy-start
  138.6 3.8 copy-start
  159.3 3.7 copy-start
  173.5 3.8 copy-start
  194.2 3.7 copy-start
  208.4 3.8 copy-start
  216.8 9.5 %all-to-all-start.8 = ((bf16[8,2,8192]{2,1,0:T(2,128)(2,1)}), bf16[8,2,8192]{2,1,0:T(2,128)(2,1)S(1)}, u32[]{:S(2)}, u32[]{:S(2)}) async-start(bf16[8,2,8192]{2,1,0:T(2,128)(2,1)} %reshape.436), calls=%async_computation.8 | async-start | bytes 524288 | tf_op jit(solution)/shard_map/all_to_all | solution.py:172
  226.3 10.0 %all-to-all-start.9 = ((bf16[8,2,8192]{2,1,0:T(2,128)(2,1)}), bf16[8,2,8192]{2,1,0:T(2,128)(2,1)S(1)}, u32[]{:S(2)}, u32[]{:S(2)}) async-start(bf16[8,2,8192]{2,1,0:T(2,128)(2,1)} %reshape.438), calls=%async_computation.9 | async-start | bytes 524288 | tf_op jit(solution)/shard_map/all_to_all | solution.py:175
  229.9 9.9 %copy-start.12 = (bf16[4,1024,1,128]{3,1,2,0:T(8,128)(2,1)S(1)}, bf16[4,1024,1,128]{3,1,2,0:T(8,128)(2,1)}, u32[]{:S(2)}) copy-start(bf16[4,1024,1,128]{3,1,2,0:T(8,128)(2,1)} %get-tuple-element.348) | copy-start | bytes 3145732
  236.2 15.3 %all-to-all-start.6 = ((bf16[1024,4,128]{2,1,0:T(4,128)(2,1)}), bf16[1024,4,128]{2,1,0:T(4,128)(2,1)S(1)}, u32[]{:S(2)}, u32[]{:S(2)}) async-start(bf16[1024,4,128]{2,1,0:T(4,128)(2,1)} %copy.153), calls=%async_computation.6 | async-start | bytes 2097152 | tf_op jit(solution)/shard_map/all_to_all | solution.py:168
  251.5 16.6 %all-to-all-start.7 = ((bf16[1024,4,128]{2,1,0:T(4,128)(2,1)}), bf16[1024,4,128]{2,1,0:T(4,128)(2,1)S(1)}, u32[]{:S(2)}, u32[]{:S(2)}) async-start(bf16[1024,4,128]{2,1,0:T(4,128)(2,1)} %bitcast.260), calls=%async_computation.7 | async-start | bytes 2097152 | tf_op jit(solution)/shard_map/all_to_all | solution.py:169
  255.4 5.0 %copy-start.9 = (f32[128,128]{1,0:T(8,128)S(1)}, f32[128,128]{1,0:T(8,128)}, u32[]{:S(2)}) copy-start(f32[128,128]{1,0:T(8,128)} %copy-done.8) | copy-start | bytes 196612
  (17 other events, 30.5 us)
where the time goes:
time: 379 us; the launch traced here: 376 us
  blocking collectives  90.5 us (24%)
  matrix products  79 us (21%)
  local copies, waits for them, and re-layouts  62 us (16%)
  waiting for transfers between devices  53.1 us (14%)
  starting transfers between devices  38.1 us (10%)
  other arithmetic  37.6 us (10%)
  loops' own time  14.1 us (4%)
    psum x1, blocking collectives, body(): lax.psum((jnp.sum(grad_query, axis=0).reshape(HQ * HD), jnp.sum(grad_key,...  90.5 us
    dot_general x8, matrix products, row_step(): jnp.einsum('hrk,kd->rhd', dscore, key_one, preferred_element_type=jnp.flo...  24.6 us
    dot_general x8, matrix products, row_step(): jnp.einsum('rhd,kd->hrk', cot_rows, value_one, preferred_element_type=jnp...  19.4 us
    dot_general x8, matrix products, row_step(): jnp.einsum('rhd,kd->hrk', query_rows, key_one, preferred_element_type=jnp...  18.6 us
    all_to_all x1, waiting for transfers between devices, body(): lax.all_to_all(outputs, 'seq', split_axis=0, concat_axis=1, tiled=True)  9.94 us
    another operation x1, loops' own time, attend(): lax.scan(head_step, (zeros_kv, zeros_kv), jnp.arange(heads // head_block,...  8.13 us
    unnamed x57, local copies, waits for them, and re-layouts  7.6 us
  transfers between devices with their start and end apart: 10, of which 10 were waited for; matrix products, arithmetic and copies ran while one was open for 7% of the time, Pallas kernels for 0%

commit v1 on v0

--- a/solution.py
+++ b/solution.py
@@ -2,6 +2,7 @@
 import jax.numpy as jnp
 from jax import lax
 from jax.sharding import PartitionSpec as P
+from jax.lax import psum
 
 HQ = 32
 KV = 4
@@ -180,13 +181,16 @@
     dv_tokens = jnp.sum(dv_copies.reshape(tokens, KV, copies, HD), axis=2)
     grad_query = rotary_back(dq_tokens.astype(jnp.float32), positions)
     grad_key = rotary_back(dk_tokens, positions)
-    sums_query, sums_key, sums_value = lax.psum(
-        (
-            jnp.sum(grad_query, axis=0).reshape(HQ * HD),
-            jnp.sum(grad_key, axis=0).reshape(KV * HD),
-            jnp.sum(dv_tokens, axis=0).reshape(KV * HD),
+    sums_query, sums_key, sums_value = psum(
+        psum(
+            (
+                jnp.sum(grad_query, axis=0).reshape(HQ * HD),
+                jnp.sum(grad_key, axis=0).reshape(KV * HD),
+                jnp.sum(dv_tokens, axis=0).reshape(KV * HD),
+            ),
+            "seq",
         ),
-        ("dp", "seq"),
+        "dp",
     )
     return (
         out_tokens.reshape(1, tokens, HQ * HD),

time: 379 us -> 472 us (1.25)
  blocking collectives: 90.5 us -> 181 us
    psum x1 -> x2, blocking collectives: 90.5 us -> 181 us  [the longest x1 156 us: body(): psum(psum((jnp.sum(grad_query, axis=0).reshape(HQ * HD), jnp.sum(grad_key...]
  transfers between devices with their start and end apart: 10 -> 10, of which waited for: 10 -> 10; matrix products, arithmetic and copies ran while one was open for 7% -> 6% of each run, Pallas kernels for 0% -> 0%
where the time goes in v1:
time: 472 us; the launch traced here: 467 us
  blocking collectives  181 us (38%)
  matrix products  78.9 us (17%)
  local copies, waits for them, and re-layouts  62 us (13%)
  waiting for transfers between devices  53.2 us (11%)
  starting transfers between devices  38.1 us (8%)
  other arithmetic  37.6 us (8%)
  loops' own time  14.1 us (3%)
    psum x1, blocking collectives, body(): psum(psum((jnp.sum(grad_query, axis=0).reshape(HQ * HD), jnp.sum(grad_key...  156 us
    psum x1, blocking collectives, body(): psum((jnp.sum(grad_query, axis=0).reshape(HQ * HD), jnp.sum(grad_key, axi...  24.9 us
    dot_general x8, matrix products, row_step(): jnp.einsum('hrk,kd->rhd', dscore, key_one, preferred_element_type=jnp.flo...  24.6 us
    dot_general x8, matrix products, row_step(): jnp.einsum('rhd,kd->hrk', cot_rows, value_one, preferred_element_type=jnp...  19.3 us
    dot_general x8, matrix products, row_step(): jnp.einsum('rhd,kd->hrk', query_rows, key_one, preferred_element_type=jnp...  18.5 us
    all_to_all x1, waiting for transfers between devices, body(): lax.all_to_all(outputs, 'seq', split_axis=0, concat_axis=1, tiled=True)  9.94 us
  transfers between devices with their start and end apart: 10, of which 10 were waited for; matrix products, arithmetic and copies ran while one was open for 6% of the time, Pallas kernels for 0%

profile of v1, /device:TPU:1, one launch (start us, length us, event | category | flops | bytes accessed | tf_op | source)
XLA Modules:
  0.0 466.6 jit_solution(10819471310725898682)
XLA Ops:
  2.4 6.5 %all-to-all-start.2 = ((bf16[128,8,128]{2,0,1:T(8,128)(2,1)}), bf16[128,8,128]{2,0,1:T(8,128)(2,1)S(1)}, u32[]{:S(2)}, u32[]{:S(2)}) async-start(bf16[128,8,128]{2,0,1:T(8,128)(2,1)} %bitcast.11), calls=%async_computation.2 | async-start | bytes 524288 | tf_op jit(solution)/shard_map/all_to_all | solution.py:159
  15.8 3.4 all-to-all-start.4
  19.3 6.0 %all-to-all-done.4 = bf16[128,8,128]{2,0,1:T(8,128)(2,1)S(1)} async-done(((bf16[128,8,128]{2,0,1:T(8,128)(2,1)}), bf16[128,8,128]{2,0,1:T(8,128)(2,1)S(1)}, u32[]{:S(2)}, u32[]{:S(2)}) %all-to-all-start.4) | async-done | bytes 262176 | tf_op jit(solution)/shard_map/all_to_all | solution.py:160
  26.1 3.4 all-to-all-start.5
  29.8 5.8 %all-to-all-done.5 = bf16[128,8,128]{2,0,1:T(8,128)(2,1)S(1)} async-done(((bf16[128,8,128]{2,0,1:T(8,128)(2,1)}), bf16[128,8,128]{2,0,1:T(8,128)(2,1)S(1)}, u32[]{:S(2)}, u32[]{:S(2)}) %all-to-all-start.5) | async-done | bytes 262176 | tf_op jit(solution)/shard_map/all_to_all | solution.py:155
  36.4 3.4 all-to-all-start.3
  41.2 4.7 %all-to-all-done.3 = bf16[128,8,128]{2,0,1:T(8,128)(2,1)S(1)} async-done(((bf16[128,8,128]{2,0,1:T(8,128)(2,1)}), bf16[128,8,128]{2,0,1:T(8,128)(2,1)S(1)}, u32[]{:S(2)}, u32[]{:S(2)}) %all-to-all-start.3) | async-done | bytes 262176 | tf_op jit(solution)/shard_map/all_to_all | solution.py:154
  45.9 3.7 all-to-all-start.1
  53.5 6.5 %all-to-all-done.1 = bf16[128,32,128]{0,2,1:T(8,128)(2,1)S(1)} async-done(((bf16[128,32,128]{0,2,1:T(8,128)(2,1)}), bf16[128,32,128]{0,2,1:T(8,128)(2,1)S(1)}, u32[]{:S(2)}, u32[]{:S(2)}) %all-to-all-start.1) | async-done | bytes 1048608 | tf_op jit(solution)/shard_map/all_to_all | solution.py:156
  60.0 3.6 all-to-all-start
  66.7 7.2 %all-to-all-done = bf16[128,32,128]{2,0,1:T(8,128)(2,1)S(1)} async-done(((bf16[128,32,128]{2,0,1:T(8,128)(2,1)}), bf16[128,32,128]{2,0,1:T(8,128)(2,1)S(1)}, u32[]{:S(2)}, u32[]{:S(2)}) %all-to-all-start) | async-done | bytes 1048608 | tf_op jit(solution)/shard_map/all_to_all | solution.py:153
  75.0 139.6 %while.59 = (s32[]{:T(128)}, f32[1024,1,128]{2,0,1:T(8,128)S(1)}, f32[1024,1,128]{2,0,1:T(8,128)S(1)}, bf16[4,1024,1,128]{3,1,2,0:T(8,128)(2,1)}, bf16[4,1024,1,...) while((s32[]{:T(128)}, f32[1024,1,128]{2,0,1:T(8,128)S(1)}, ...), condition=%wide.region_6.7_spmd.clone.clone, body=%wide.region_0.6_spmd.clone.clone.sunk | while | flops 1359287296 | bytes 49224388 | solution.py:117
  79.6 28.5 %while.60 = (s32[]{:T(128)}, f32[1024,128]{1,0:T(8,128)S(1)}, f32[1024,128]{1,0:T(8,128)S(1)}, bf16[2,512,1,128]{3,1,0,2:T(8,128)(2,1)}, bf16[2,512,1,128]{3,1,2...) while((s32[]{:T(128)}, f32[1024,128]{1,0:T(8,128)S(1)}, ...), condition=%wide.region_5.5_spmd.clone.clone, body=%wide.region_1.4_spmd.clone.clone.sunk | while | flops 1359025152 | bytes 41875732 | solution.py:105
  90.1 3.1 fusion.81
  104.3 3.1 fusion.81
  114.5 28.5 %while.60 = (s32[]{:T(128)}, f32[1024,128]{1,0:T(8,128)S(1)}, f32[1024,128]{1,0:T(8,128)S(1)}, bf16[2,512,1,128]{3,1,0,2:T(8,128)(2,1)}, bf16[2,512,1,128]{3,1,2...) while((s32[]{:T(128)}, f32[1024,128]{1,0:T(8,128)S(1)}, ...), condition=%wide.region_5.5_spmd.clone.clone, body=%wide.region_1.4_spmd.clone.clone.sunk | while | flops 1359025152 | bytes 41875732 | solution.py:105
  139.2 3.1 fusion.81
  149.3 28.5 %while.60 = (s32[]{:T(128)}, f32[1024,128]{1,0:T(8,128)S(1)}, f32[1024,128]{1,0:T(8,128)S(1)}, bf16[2,512,1,128]{3,1,0,2:T(8,128)(2,1)}, bf16[2,512,1,128]{3,1,2...) while((s32[]{:T(128)}, f32[1024,128]{1,0:T(8,128)S(1)}, ...), condition=%wide.region_5.5_spmd.clone.clone, body=%wide.region_1.4_spmd.clone.clone.sunk | while | flops 1359025152 | bytes 41875732 | solution.py:105
  174.1 3.1 fusion.81
  184.2 28.5 %while.60 = (s32[]{:T(128)}, f32[1024,128]{1,0:T(8,128)S(1)}, f32[1024,128]{1,0:T(8,128)S(1)}, bf16[2,512,1,128]{3,1,0,2:T(8,128)(2,1)}, bf16[2,512,1,128]{3,1,2...) while((s32[]{:T(128)}, f32[1024,128]{1,0:T(8,128)S(1)}, ...), condition=%wide.region_5.5_spmd.clone.clone, body=%wide.region_1.4_spmd.clone.clone.sunk | while | flops 1359025152 | bytes 41875732 | solution.py:105
  209.0 3.1 fusion.81
  216.7 3.4 all-to-all-start.8
  221.8 4.5 all-to-all-done.8
  226.2 3.6 all-to-all-start.9
  229.8 3.1 copy.153
  232.9 3.2 all-to-all-done.9
  236.2 3.6 all-to-all-start.6
  241.5 9.9 %all-to-all-done.6 = bf16[1024,4,128]{2,1,0:T(4,128)(2,1)S(1)} async-done(((bf16[1024,4,128]{2,1,0:T(4,128)(2,1)}), bf16[1024,4,128]{2,1,0:T(4,128)(2,1)S(1)}, u32[]{:S(2)}, u32[]{:S(2)}) %all-to-all-start.6) | async-done | bytes 1048608 | tf_op jit(solution)/shard_map/all_to_all | solution.py:169
  251.5 3.6 all-to-all-start.7
  273.0 3.2 copy.163
  285.9 24.9 %all-reduce.1 = (f32[4096]{0:T(1024)S(1)}, f32[512]{0:T(512)S(1)}, f32[512]{0:T(512)S(1)}) all-reduce(f32[4096]{0:T(1024)S(1)} %bitcast.274, f32[512]{0:T(512)S(1)} %bitcast.276, f32[512]{0:T(512)S(1)} %bitcast.277), channel_id=1, replica_groups=mesh['dp'=32,'seq'=8] {'seq'}, use_global_device_ids=true, to_apply=%region_10.11 | all-reduce | flops 5120 | bytes 40960 | tf_op jit(solution)/shard_map/psum | solution.py:185
  310.8 155.8 %all-reduce = (f32[4096]{0:T(1024)}, f32[512]{0:T(512)}, f32[512]{0:T(512)}) all-reduce(f32[4096]{0:T(1024)S(1)} %get-tuple-element.712, f32[512]{0:T(512)S(1)} %get-tuple-element.713, f32[512]{0:T(512)S(1)} %get-tuple-element.714), channel_id=1, replica_groups=mesh['dp'=32,'seq'=8] {'dp'}, use_global_device_ids=true, to_apply=%region_11.12 | all-reduce | flops 5120 | bytes 40960 | tf_op jit(solution)/shard_map/psum | solution.py:184
  (323 shorter events, 162.3 us)
Async XLA Ops:
  0.6 10.7 %copy-start.22 = (bf16[1,128,512]{2,1,0:T(8,128)(2,1)S(1)}, bf16[1,128,512]{2,1,0:T(8,128)(2,1)}, u32[]{:S(2)}) copy-start(bf16[1,128,512]{2,1,0:T(8,128)(2,1)} %param.15) | copy-start | bytes 393220
  0.6 10.9 %copy-start.23 = (bf16[1,128,512]{2,1,0:T(8,128)(2,1)S(1)}, bf16[1,128,512]{2,1,0:T(8,128)(2,1)}, u32[]{:S(2)}) copy-start(bf16[1,128,512]{2,1,0:T(8,128)(2,1)} %param.18) | copy-start | bytes 393220
  2.4 16.9 %copy-start.25 = (bf16[512]{0:T(512)(128)(2,1)S(1)}, bf16[512]{0:T(512)(128)(2,1)}, u32[]{:S(2)}) copy-start(bf16[512]{0:T(512)(128)(2,1)} %param.20) | copy-start | bytes 3076
  2.4 12.7 %all-to-all-start.2 = ((bf16[128,8,128]{2,0,1:T(8,128)(2,1)}), bf16[128,8,128]{2,0,1:T(8,128)(2,1)S(1)}, u32[]{:S(2)}, u32[]{:S(2)}) async-start(bf16[128,8,128]{2,0,1:T(8,128)(2,1)} %bitcast.11), calls=%async_computation.2 | async-start | bytes 524288 | tf_op jit(solution)/shard_map/all_to_all | solution.py:159
  12.1 37.5 %copy-start.8 = (f32[128,128]{1,0:T(8,128)}, f32[128,128]{1,0:T(8,128)S(1)}, u32[]{:S(2)}) copy-start(f32[128,128]{1,0:T(8,128)S(1)} %get-tuple-element.738) | copy-start | bytes 196612
  12.1 37.6 %copy-start.6 = (f32[128,128]{1,0:T(8,128)}, f32[128,128]{1,0:T(8,128)S(1)}, u32[]{:S(2)}) copy-start(f32[128,128]{1,0:T(8,128)S(1)} %get-tuple-element.737) | copy-start | bytes 196612
  15.8 9.5 %all-to-all-start.4 = ((bf16[128,8,128]{2,0,1:T(8,128)(2,1)}), bf16[128,8,128]{2,0,1:T(8,128)(2,1)S(1)}, u32[]{:S(2)}, u32[]{:S(2)}) async-start(bf16[128,8,128]{2,0,1:T(8,128)(2,1)} %bitcast.21), calls=%async_computation.4 | async-start | bytes 524288 | tf_op jit(solution)/shard_map/all_to_all | solution.py:160
  19.3 20.5 %copy-start.10 = (bf16[1,128,4096]{2,1,0:T(8,128)(2,1)S(1)}, bf16[1,128,4096]{2,1,0:T(8,128)(2,1)}, u32[]{:S(2)}) copy-start(bf16[1,128,4096]{2,1,0:T(8,128)(2,1)} %param.23) | copy-start | bytes 3145732
  25.3 15.8 %copy-start.13 = (bf16[128,8,128]{2,0,1:T(8,128)(2,1)}, bf16[128,8,128]{2,0,1:T(8,128)(2,1)S(1)}, u32[]{:S(2)}) copy-start(bf16[128,8,128]{2,0,1:T(8,128)(2,1)S(1)} %all-to-all-done.4) | copy-start | bytes 786436
  26.1 9.5 %all-to-all-start.5 = ((bf16[128,8,128]{2,0,1:T(8,128)(2,1)}), bf16[128,8,128]{2,0,1:T(8,128)(2,1)S(1)}, u32[]{:S(2)}, u32[]{:S(2)}) async-start(bf16[128,8,128]{2,0,1:T(8,128)(2,1)} %bitcast.26), calls=%async_computation.5 | async-start | bytes 524288 | tf_op jit(solution)/shard_map/all_to_all | solution.py:155
  36.4 9.5 %all-to-all-start.3 = ((bf16[128,8,128]{2,0,1:T(8,128)(2,1)}), bf16[128,8,128]{2,0,1:T(8,128)(2,1)S(1)}, u32[]{:S(2)}, u32[]{:S(2)}) async-start(bf16[128,8,128]{2,0,1:T(8,128)(2,1)} %bitcast.17), calls=%async_computation.3 | async-start | bytes 524288 | tf_op jit(solution)/shard_map/all_to_all | solution.py:154
  39.8 10.0 %copy-start.11 = (bf16[1,128,4096]{2,1,0:T(8,128)(2,1)S(1)}, bf16[1,128,4096]{2,1,0:T(8,128)(2,1)}, u32[]{:S(2)}) copy-start(bf16[1,128,4096]{2,1,0:T(8,128)(2,1)} %param.14) | copy-start | bytes 3145732
  45.9 3.8 copy-start.17
  45.9 4.6 copy-start.24
  45.9 14.1 %all-to-all-start.1 = ((bf16[128,32,128]{0,2,1:T(8,128)(2,1)}), bf16[128,32,128]{0,2,1:T(8,128)(2,1)S(1)}, u32[]{:S(2)}, u32[]{:S(2)}) async-start(bf16[128,32,128]{0,2,1:T(8,128)(2,1)} %bitcast.6), calls=%async_computation.1 | async-start | bytes 2097152 | tf_op jit(solution)/shard_map/all_to_all | solution.py:156
  52.2 11.4 %copy-start.14 = (bf16[128,8,128]{2,0,1:T(8,128)(2,1)S(1)}, bf16[128,8,128]{2,0,1:T(8,128)(2,1)}, u32[]{:S(2)}) copy-start(bf16[128,8,128]{2,0,1:T(8,128)(2,1)} %copy-done.13) | copy-start | bytes 786436
  52.2 11.4 %copy-start.16 = (bf16[128,8,128]{2,0,1:T(8,128)(2,1)S(1)}, bf16[128,8,128]{2,0,1:T(8,128)(2,1)}, u32[]{:S(2)}) copy-start(bf16[128,8,128]{2,0,1:T(8,128)(2,1)} %copy-done.15) | copy-start | bytes 786436
  60.0 13.9 %all-to-all-start = ((bf16[128,32,128]{2,0,1:T(8,128)(2,1)}), bf16[128,32,128]{2,0,1:T(8,128)(2,1)S(1)}, u32[]{:S(2)}, u32[]{:S(2)}) async-start(bf16[128,32,128]{2,0,1:T(8,128)(2,1)} %copy.142), calls=%async_computation | async-start | bytes 2097152 | tf_op jit(solution)/shard_map/all_to_all | solution.py:153
  89.4 3.7 copy-start
  103.7 3.7 copy-start
  124.3 3.7 copy-start
  138.6 3.7 copy-start
  159.2 3.7 copy-start
  173.5 3.7 copy-start
  194.1 3.7 copy-start
  208.4 3.7 copy-start
  216.7 9.5 %all-to-all-start.8 = ((bf16[8,2,8192]{2,1,0:T(2,128)(2,1)}), bf16[8,2,8192]{2,1,0:T(2,128)(2,1)S(1)}, u32[]{:S(2)}, u32[]{:S(2)}) async-start(bf16[8,2,8192]{2,1,0:T(2,128)(2,1)} %reshape.436), calls=%async_computation.8 | async-start | bytes 524288 | tf_op jit(solution)/shard_map/all_to_all | solution.py:173
  226.2 10.0 %all-to-all-start.9 = ((bf16[8,2,8192]{2,1,0:T(2,128)(2,1)}), bf16[8,2,8192]{2,1,0:T(2,128)(2,1)S(1)}, u32[]{:S(2)}, u32[]{:S(2)}) async-start(bf16[8,2,8192]{2,1,0:T(2,128)(2,1)} %reshape.438), calls=%async_computation.9 | async-start | bytes 524288 | tf_op jit(solution)/shard_map/all_to_all | solution.py:176
  229.8 9.9 %copy-start.12 = (bf16[4,1024,1,128]{3,1,2,0:T(8,128)(2,1)S(1)}, bf16[4,1024,1,128]{3,1,2,0:T(8,128)(2,1)}, u32[]{:S(2)}) copy-start(bf16[4,1024,1,128]{3,1,2,0:T(8,128)(2,1)} %get-tuple-element.348) | copy-start | bytes 3145732
  236.2 15.3 %all-to-all-start.6 = ((bf16[1024,4,128]{2,1,0:T(4,128)(2,1)}), bf16[1024,4,128]{2,1,0:T(4,128)(2,1)S(1)}, u32[]{:S(2)}, u32[]{:S(2)}) async-start(bf16[1024,4,128]{2,1,0:T(4,128)(2,1)} %copy.153), calls=%async_computation.6 | async-start | bytes 2097152 | tf_op jit(solution)/shard_map/all_to_all | solution.py:169
  251.5 16.6 %all-to-all-start.7 = ((bf16[1024,4,128]{2,1,0:T(4,128)(2,1)}), bf16[1024,4,128]{2,1,0:T(4,128)(2,1)S(1)}, u32[]{:S(2)}, u32[]{:S(2)}) async-start(bf16[1024,4,128]{2,1,0:T(4,128)(2,1)} %bitcast.260), calls=%async_computation.7 | async-start | bytes 2097152 | tf_op jit(solution)/shard_map/all_to_all | solution.py:170
  255.4 5.0 %copy-start.9 = (f32[128,128]{1,0:T(8,128)S(1)}, f32[128,128]{1,0:T(8,128)}, u32[]{:S(2)}) copy-start(f32[128,128]{1,0:T(8,128)} %copy-done.8) | copy-start | bytes 196612
  (17 other events, 30.5 us)
